TPU v7x, 32 devices: a whole 2x2x4 slice. The times are simulated.
32 devices in a mesh: ctx: 8 (over z, y), tp: 4 (over x, core).
Axes of the slice: x: 2, y: 2, z: 4, core: 2. Of those that a mesh axis runs over, the one named last changes fastest.
Arguments:
- layer_inputs: bfloat16 [1536, 2048], P('ctx', 'tp'), may hold values from -6 to 6
- states: float32 [1536, 2048], P('ctx', 'tp'), may hold values from -0.7 to 0.7
- cotangent: float32 [1536, 2048], P('ctx', 'tp'), may hold values from -0.009765625 to 0.009765625
- block_weights: float32 [32, 64, 64], P('tp'), may hold values from -1 to 1
Outputs:
- grad_proj: float32 [2048, 2048], P(('ctx', 'tp'))
All inputs are finite; a program needn't handle non-finite values.
Results may differ from a plain program's by a relative error of at most 0.0029.
Values may be sent and summed in bfloat16 or wider, within the bound.
A program may use at most 64 MiB of HBM per device.

v0:
```python
import jax
import jax.numpy as jnp
from jax import lax
from jax.sharding import PartitionSpec as P

exact = lax.Precision.HIGHEST


def from_behind(value, axis, by):
    size = lax.axis_size(axis)
    pairs = [(i, i + by) for i in range(size) if 0 <= i + by < size]
    return lax.ppermute(value, axis, pairs)


def compose(right_map, left_map):
    right_mat, right_vec = right_map
    left_mat, left_vec = left_map
    joined = jnp.einsum("hisj,hjsk->hisk", left_mat, right_mat, precision=exact)
    shifted = left_vec + jnp.einsum("hisj,hjs->his", left_mat, right_vec, precision=exact)
    return (joined, shifted)


def on_device(layer_inputs, states, cotangent, block_weights):
    tokens_here = states.shape[0]
    head_local = block_weights.shape[0]
    head_width = block_weights.shape[1]
    block_len = 32
    blocks = tokens_here // block_len

    def arrange(values):
        shaped = values.reshape(blocks, block_len, head_local, head_width)
        return jnp.transpose(shaped, (1, 2, 3, 0))

    slopes = arrange(1.0 - states * states)
    upstream = arrange(cotangent)

    def build_step(affine_maps, pieces):
        matrices, offsets = affine_maps
        slope_now, grad_now = pieces
        pulled = jnp.einsum("hji,hjsk->hisk", block_weights, matrices, precision=exact)
        matrices = slope_now[..., None] * pulled
        offsets = slope_now * (
            grad_now + jnp.einsum("hji,hjs->his", block_weights, offsets, precision=exact)
        )
        return ((matrices, offsets), None)

    identity_mats = jnp.broadcast_to(
        jnp.eye(head_width, dtype=jnp.float32)[None, :, None, :],
        (head_local, head_width, blocks, head_width),
    )
    zero_offsets = jnp.zeros((head_local, head_width, blocks), jnp.float32)
    (matrices, offsets), unused = lax.scan(
        build_step, (identity_mats, zero_offsets), (slopes, upstream), reverse=True
    )
    flipped = (jnp.flip(matrices, 2), jnp.flip(offsets, 2))
    suffix = lax.associative_scan(compose, flipped, axis=2)
    suffix_mat = jnp.flip(suffix[0], 2)
    suffix_vec = jnp.flip(suffix[1], 2)
    device_mat = suffix_mat[:, :, :1, :]
    device_vec = suffix_vec[:, :, :1]

    def relay_turn(step_index, entering):
        leaving = device_vec + jnp.einsum("hisj,hjs->his", device_mat, entering, precision=exact)
        return from_behind(leaving, "ctx", -1)

    entering = lax.fori_loop(0, lax.axis_size("ctx") - 1, relay_turn, jnp.zeros_like(device_vec))
    later_mat = suffix_mat[:, :, 1:, :]
    later_vector = suffix_vec[:, :, 1:]
    inner_starts = later_vector + jnp.einsum(
        "hisj,hj->his", later_mat, entering[:, :, 0], precision=exact
    )
    starts = jnp.concatenate([inner_starts, entering], axis=2)

    def solve_step(subsequent_step, pieces):
        slope_now, grad_now = pieces
        current = slope_now * (
            grad_now + jnp.einsum("hji,hjs->his", block_weights, subsequent_step, precision=exact)
        )
        return (current, current)

    remaining_part, adjoints = lax.scan(solve_step, starts, (slopes, upstream), reverse=True)
    adjoint_bf = (
        jnp.transpose(adjoints, (1, 2, 3, 0))
        .reshape(head_local * head_width, tokens_here)
        .astype(jnp.bfloat16)
    )
    gathered = lax.all_gather(layer_inputs, "tp", axis=1, tiled=True)
    summed = lax.psum_scatter(
        lax.dot_general(
            gathered, adjoint_bf, (((0,), (1,)), ((), ())), preferred_element_type=jnp.float32
        ),
        "ctx",
        scatter_dimension=0,
        tiled=True,
    )
    result = lax.all_to_all(summed, "tp", split_axis=0, concat_axis=1, tiled=True)
    return result


def solution(mesh):
    in_specs = (P("ctx", "tp"), P("ctx", "tp"), P("ctx", "tp"), P("tp", None, None))
    out_specs = P(("ctx", "tp"), None)
    return jax.shard_map(
        on_device, mesh=mesh, in_specs=in_specs, out_specs=out_specs, check_vma=False
    )
```

profile of v0, /device:TPU:0, one launch (start us, length us, event | category | flops | bytes accessed | tf_op | source)
XLA Modules:
  0.0 375.9 jit_solution(12649809995185188845)
XLA Ops:
  11.1 115.7 %while.45 = (s32[]{:T(128)}, f32[8,64,6,64]{3,1,2,0:T(8,128)S(1)}, f32[8,64,6]{1,2,0:T(8,128)S(1)}, f32[32,8,64,6]{2,3,1,0:T(8,128)}, f32[8,64,64]{2,1,0:T(8,128...) while((s32[]{:T(128)}, f32[8,64,6,64]{3,1,2,0:T(8,128)S(1)}, ...), condition=%wide.region_1.2_spmd.clone, body=%wide.region_0.1_spmd.clone.sunk | while | flops 153560064 | bytes 3518595 | solution.py:52
  12.0 1.5 convolution_multiply_fusion.2
  19.3 1.5 convolution_multiply_fusion.2
  30.1 1.5 convolution_multiply_fusion.2
  41.0 1.5 convolution_multiply_fusion.2
  51.8 1.5 convolution_multiply_fusion.2
  62.7 1.5 convolution_multiply_fusion.2
  69.9 1.5 convolution_multiply_fusion.2
  80.7 1.5 convolution_multiply_fusion.2
  91.6 1.5 convolution_multiply_fusion.2
  102.4 1.5 convolution_multiply_fusion.2
  113.3 1.5 convolution_multiply_fusion.2
  124.1 1.5 convolution_multiply_fusion.2
  132.9 8.5 %pad.66 = f32[8,64,5,64]{1,3,2,0:T(8,128)} pad(f32[8,64,3,64]{1,3,2,0:T(8,128)S(1)} %pad_add_fusion, f32[]{:T(128)} %constant.84.clone.1), padding=0_0_0x0_0_0x0_0_1x0_0_0 | pad | bytes 1048580
  141.4 8.6 %pad.33 = f32[8,64,6,64]{1,3,2,0:T(8,128)} pad(f32[8,64,3,64]{1,3,2,0:T(8,128)S(1)} %pad_add_fusion, f32[]{:T(128)} %constant.84.clone.1), padding=0_0_0x0_0_0x1_0_1x0_0_0 | pad | bytes 1179652 | tf_op jit(solution)/shard_map/pad | solution.py:56
  150.0 1.8 convolution_bitcast_fusion.2
  151.7 1.6 copy.30
  155.7 8.5 %pad.32 = f32[8,64,6,64]{1,3,2,0:T(8,128)} pad(f32[8,64,3,64]{1,3,2,0:T(8,128)S(1)} %pad_maximum_fusion, f32[]{:T(128)} %constant.84.clone.1), padding=0_0_0x0_0_0x0_1_1x0_0_0 | pad | bytes 1179652 | tf_op jit(solution)/shard_map/pad | solution.py:56
  165.9 48.5 %while.43 = (s32[]{:T(128)}, f32[8,64,1]{1,0,2:T(8,128)S(1)}, f32[8,64,1]{1,2,0:T(1,128)S(1)}, f32[8,64,1,64]{3,2,1,0:T(1,128)S(1)}, s32[]{:T(128)}) while((s32[]{:T(128)}, f32[8,64,1]{1,0,2:T(8,128)S(1)}, f32[8,64,1]{1,2,0:T(1,128)S(1)}, f32[8,64,1,64]{3,2,1,0:T(1,128)S(1)}, s32[]{:T(128)}) %tuple.93), condition=%wide.region_3.4_spmd, body=%wide.region_2.3_spmd.sunk | while | flops 393730 | bytes 149605 | solution.py:66
  167.8 5.2 %collective-permute-done = f32[8,64,1]{1,0,2:T(8,128)S(1)} collective-permute-done((f32[8,64,1]{1,0,2:T(8,128)S(1)}, f32[8,64,1]{1,0,2:T(8,128)S(1)}, u32[]{:S(2)}, u32[]{:S(2)}) %collective-permute-start) | collective-permute-done | bytes 2080 | tf_op jit(solution)/shard_map/while/body/eval_jaxpr/ppermute | solution.py:12
  174.8 5.1 %collective-permute-done = f32[8,64,1]{1,0,2:T(8,128)S(1)} collective-permute-done((f32[8,64,1]{1,0,2:T(8,128)S(1)}, f32[8,64,1]{1,0,2:T(8,128)S(1)}, u32[]{:S(2)}, u32[]{:S(2)}) %collective-permute-start) | collective-permute-done | bytes 2080 | tf_op jit(solution)/shard_map/while/body/eval_jaxpr/ppermute | solution.py:12
  181.7 5.1 %collective-permute-done = f32[8,64,1]{1,0,2:T(8,128)S(1)} collective-permute-done((f32[8,64,1]{1,0,2:T(8,128)S(1)}, f32[8,64,1]{1,0,2:T(8,128)S(1)}, u32[]{:S(2)}, u32[]{:S(2)}) %collective-permute-start) | collective-permute-done | bytes 2080 | tf_op jit(solution)/shard_map/while/body/eval_jaxpr/ppermute | solution.py:12
  188.6 5.1 %collective-permute-done = f32[8,64,1]{1,0,2:T(8,128)S(1)} collective-permute-done((f32[8,64,1]{1,0,2:T(8,128)S(1)}, f32[8,64,1]{1,0,2:T(8,128)S(1)}, u32[]{:S(2)}, u32[]{:S(2)}) %collective-permute-start) | collective-permute-done | bytes 2080 | tf_op jit(solution)/shard_map/while/body/eval_jaxpr/ppermute | solution.py:12
  195.5 5.1 %collective-permute-done = f32[8,64,1]{1,0,2:T(8,128)S(1)} collective-permute-done((f32[8,64,1]{1,0,2:T(8,128)S(1)}, f32[8,64,1]{1,0,2:T(8,128)S(1)}, u32[]{:S(2)}, u32[]{:S(2)}) %collective-permute-start) | collective-permute-done | bytes 2080 | tf_op jit(solution)/shard_map/while/body/eval_jaxpr/ppermute | solution.py:12
  202.4 5.1 %collective-permute-done = f32[8,64,1]{1,0,2:T(8,128)S(1)} collective-permute-done((f32[8,64,1]{1,0,2:T(8,128)S(1)}, f32[8,64,1]{1,0,2:T(8,128)S(1)}, u32[]{:S(2)}, u32[]{:S(2)}) %collective-permute-start) | collective-permute-done | bytes 2080 | tf_op jit(solution)/shard_map/while/body/eval_jaxpr/ppermute | solution.py:12
  209.4 5.1 %collective-permute-done = f32[8,64,1]{1,0,2:T(8,128)S(1)} collective-permute-done((f32[8,64,1]{1,0,2:T(8,128)S(1)}, f32[8,64,1]{1,0,2:T(8,128)S(1)}, u32[]{:S(2)}, u32[]{:S(2)}) %collective-permute-start) | collective-permute-done | bytes 2080 | tf_op jit(solution)/shard_map/while/body/eval_jaxpr/ppermute | solution.py:12
  214.5 2.2 fusion.24
  217.5 37.3 %while.44 = (s32[]{:T(128)}, f32[8,64,6]{1,2,0:T(8,128)S(1)}, bf16[32,8,64,6]{2,3,1,0:T(8,128)(2,1)S(1)}, f32[32,8,64,6]{2,3,1,0:T(8,128)}, f32[32,8,64,6]{2,3,1...) while((s32[]{:T(128)}, f32[8,64,6]{1,2,0:T(8,128)S(1)}, ...), condition=%wide.region_5.6_spmd, body=%wide.region_4.5_spmd.sunk | while | flops 2365443 | bytes 409709 | solution.py:81
  255.1 8.6 %all_gather.3 = bf16[192,2048]{1,0:T(8,128)(2,1)S(1)} all-gather(bf16[192,512]{1,0:T(8,128)(2,1)S(1)} %copy-done.4), channel_id=1, replica_groups=mesh['ctx'=8,'tp'=4] {'tp'}, dimensions={1}, use_global_device_ids=true | all-gather | bytes 983040 | tf_op jit(solution)/shard_map/all_gather | solution.py:87
  263.7 2.7 convolution_bitcast_fusion
  266.5 89.2 %reduce-scatter.2.cloned.1.call-done = f32[256,512]{0,1:T(8,128)} async-done(((f32[2048,512]{0,1:T(8,128)}), f32[256,512]{0,1:T(8,128)}) %reduce-scatter.2.cloned.1.call-update) | async-done | bytes 524304 | tf_op jit(solution)/shard_map/reduce_scatter | solution.py:88
  356.9 11.4 %all_to_all.19 = f32[4,64,512]{2,1,0:T(8,128)S(1)} all-to-all(f32[4,64,512]{2,1,0:T(8,128)S(1)} %bitcast.157), channel_id=1, replica_groups=mesh['ctx'=8,'tp'=4] {'tp'}, dimensions={0} | all-to-all | bytes 1048576 | tf_op jit(solution)/shard_map/all_to_all | solution.py:96
  (304 shorter events, 163.0 us)
Async XLA Ops:
  6.5 349.1 %reduce-scatter.2.cloned.1.call-start = ((), (), s32[]{:S(2)}) async-start(), calls=%async_computation.2 | async-start | bytes 4718592 | tf_op jit(solution)/shard_map/reduce_scatter | solution.py:88
  7.6 1.7 copy-start.3
  9.4 1.6 copy-start
  130.6 1.1 copy-start.2
  151.7 1.6 slice-start.1
  153.4 1.3 slice-start
  155.7 8.5 %copy-start.1 = (f32[8,64,6,64]{1,3,2,0:T(8,128)S(1)}, f32[8,64,6,64]{1,3,2,0:T(8,128)}, u32[]{:S(2)}) copy-start(f32[8,64,6,64]{1,3,2,0:T(8,128)} %pad.33) | copy-start | bytes 2359300
  166.5 6.5 %collective-permute-start = (f32[8,64,1]{1,0,2:T(8,128)S(1)}, f32[8,64,1]{1,0,2:T(8,128)S(1)}, u32[]{:S(2)}, u32[]{:S(2)}) collective-permute-start(f32[8,64,1]{1,0,2:T(8,128)S(1)} %add_bitcast_fusion.2), channel_id=1, source_target_pairs={{4,0},{8,4},{12,8},{16,12},{20,16},{24,20},{28,24},{5,1},{9,5},{13... | collective-permute-start | bytes 6152 | tf_op jit(solution)/shard_map/while/body/eval_jaxpr/ppermute | solution.py:12
  173.4 6.4 %collective-permute-start = (f32[8,64,1]{1,0,2:T(8,128)S(1)}, f32[8,64,1]{1,0,2:T(8,128)S(1)}, u32[]{:S(2)}, u32[]{:S(2)}) collective-permute-start(f32[8,64,1]{1,0,2:T(8,128)S(1)} %add_bitcast_fusion.2), channel_id=1, source_target_pairs={{4,0},{8,4},{12,8},{16,12},{20,16},{24,20},{28,24},{5,1},{9,5},{13... | collective-permute-start | bytes 6152 | tf_op jit(solution)/shard_map/while/body/eval_jaxpr/ppermute | solution.py:12
  180.4 6.4 %collective-permute-start = (f32[8,64,1]{1,0,2:T(8,128)S(1)}, f32[8,64,1]{1,0,2:T(8,128)S(1)}, u32[]{:S(2)}, u32[]{:S(2)}) collective-permute-start(f32[8,64,1]{1,0,2:T(8,128)S(1)} %add_bitcast_fusion.2), channel_id=1, source_target_pairs={{4,0},{8,4},{12,8},{16,12},{20,16},{24,20},{28,24},{5,1},{9,5},{13... | collective-permute-start | bytes 6152 | tf_op jit(solution)/shard_map/while/body/eval_jaxpr/ppermute | solution.py:12
  187.3 6.4 %collective-permute-start = (f32[8,64,1]{1,0,2:T(8,128)S(1)}, f32[8,64,1]{1,0,2:T(8,128)S(1)}, u32[]{:S(2)}, u32[]{:S(2)}) collective-permute-start(f32[8,64,1]{1,0,2:T(8,128)S(1)} %add_bitcast_fusion.2), channel_id=1, source_target_pairs={{4,0},{8,4},{12,8},{16,12},{20,16},{24,20},{28,24},{5,1},{9,5},{13... | collective-permute-start | bytes 6152 | tf_op jit(solution)/shard_map/while/body/eval_jaxpr/ppermute | solution.py:12
  194.2 6.4 %collective-permute-start = (f32[8,64,1]{1,0,2:T(8,128)S(1)}, f32[8,64,1]{1,0,2:T(8,128)S(1)}, u32[]{:S(2)}, u32[]{:S(2)}) collective-permute-start(f32[8,64,1]{1,0,2:T(8,128)S(1)} %add_bitcast_fusion.2), channel_id=1, source_target_pairs={{4,0},{8,4},{12,8},{16,12},{20,16},{24,20},{28,24},{5,1},{9,5},{13... | collective-permute-start | bytes 6152 | tf_op jit(solution)/shard_map/while/body/eval_jaxpr/ppermute | solution.py:12
  201.1 6.4 %collective-permute-start = (f32[8,64,1]{1,0,2:T(8,128)S(1)}, f32[8,64,1]{1,0,2:T(8,128)S(1)}, u32[]{:S(2)}, u32[]{:S(2)}) collective-permute-start(f32[8,64,1]{1,0,2:T(8,128)S(1)} %add_bitcast_fusion.2), channel_id=1, source_target_pairs={{4,0},{8,4},{12,8},{16,12},{20,16},{24,20},{28,24},{5,1},{9,5},{13... | collective-permute-start | bytes 6152 | tf_op jit(solution)/shard_map/while/body/eval_jaxpr/ppermute | solution.py:12
  208.1 6.4 %collective-permute-start = (f32[8,64,1]{1,0,2:T(8,128)S(1)}, f32[8,64,1]{1,0,2:T(8,128)S(1)}, u32[]{:S(2)}, u32[]{:S(2)}) collective-permute-start(f32[8,64,1]{1,0,2:T(8,128)S(1)} %add_bitcast_fusion.2), channel_id=1, source_target_pairs={{4,0},{8,4},{12,8},{16,12},{20,16},{24,20},{28,24},{5,1},{9,5},{13... | collective-permute-start | bytes 6152 | tf_op jit(solution)/shard_map/while/body/eval_jaxpr/ppermute | solution.py:12
  217.5 37.6 %copy-start.4 = (bf16[192,512]{1,0:T(8,128)(2,1)S(1)}, bf16[192,512]{1,0:T(8,128)(2,1)}, u32[]{:S(2)}) copy-start(bf16[192,512]{1,0:T(8,128)(2,1)} %param.10) | copy-start | bytes 589828
Sparse Core Ops, SparseCore 0:
  266.6 88.9 reduce-scatter.1
where the time goes:
time: 383 us; the launch traced here: 376 us
  matrix products  136 us (36%)
  waiting for transfers between devices  125 us (33%)
  local copies, waits for them, and re-layouts  65 us (17%)
  blocking collectives  20 us (5%)
  between operations  13.7 us (4%)
  starting transfers between devices  9.06 us (2%)
  other arithmetic  4.9 us (1%)
    reduce_scatter x1, waiting for transfers between devices, on_device(): lax.psum_scatter(lax.dot_general(gathered, adjoint_bf, (((0,), (1,)), (()...  89.2 us
    dot_general x32, matrix products, build_step(): jnp.einsum('hji,hjsk->hisk', block_weights, matrices, precision=exact)  48.4 us
    dot_general x32, matrix products, solve_step(): jnp.einsum('hji,hjs->his', block_weights, subsequent_step, precision=exact)  36.3 us
    dot_general x32, matrix products, build_step(): jnp.einsum('hji,hjs->his', block_weights, offsets, precision=exact)  36.1 us
    ppermute x7, waiting for transfers between devices, from_behind(): return lax.ppermute(value, axis, pairs)  35.7 us
    mul x32, local copies, waits for them, and re-layouts, build_step(): matrices = slope_now[..., None] * pulled  24.5 us
    pad x6, local copies, waits for them, and re-layouts, on_device(): suffix = lax.associative_scan(compose, flipped, axis=2)  17.5 us
    unnamed x14, local copies, waits for them, and re-layouts  11.5 us
  transfers between devices with their start and end apart: 8, of which 8 were waited for; matrix products, arithmetic and copies ran while one was open for 0% of the time, Pallas kernels for 0%

commit v1 on v0

--- a/solution.py
+++ b/solution.py
@@ -84,7 +84,26 @@
         .reshape(head_local * head_width, tokens_here)
         .astype(jnp.bfloat16)
     )
-    gathered = lax.all_gather(layer_inputs, "tp", axis=1, tiled=True)
+    back, heard, now = (lax.axis_size("tp"), lax.axis_index("tp"), layer_inputs.shape[1])
+    rack = tuple((rr * back if q == 1 else rr for q, rr in enumerate(layer_inputs.shape)))
+    gathered = lax.dynamic_update_slice_in_dim(
+        jnp.zeros(rack, layer_inputs.dtype), layer_inputs, heard * now, axis=1
+    )
+    moved = z1 = layer_inputs
+    for c in range(1, back // 2 + 1):
+        moved = lax.ppermute(
+            moved, axis_name="tp", perm=tuple(((q, (q + 1) % back) for q in range(back)))
+        )
+        gathered = lax.dynamic_update_slice_in_dim(
+            gathered, moved, (heard - c) % back * now, axis=1
+        )
+        if 2 * c < back:
+            z1 = lax.ppermute(
+                z1, axis_name="tp", perm=tuple(((q, (q - 1) % back) for q in range(back)))
+            )
+            gathered = lax.dynamic_update_slice_in_dim(
+                gathered, z1, (heard + c) % back * now, axis=1
+            )
     summed = lax.psum_scatter(
         lax.dot_general(
             gathered, adjoint_bf, (((0,), (1,)), ((), ())), preferred_element_type=jnp.float32

time: 383 us -> 354 us (0.924)
  local copies, waits for them, and re-layouts: 65 us -> 40.2 us
  blocking collectives: 20 us -> 12.3 us
    mul x32, local copies, waits for them, and re-layouts: 24.5 us -> 0.24 us  [build_step(): matrices = slope_now[..., None] * pulled]
    all_gather x1 -> x0, blocking collectives: 8.6 us -> none  [on_device(): gathered = lax.all_gather(layer_inputs, 'tp', axis=1, tiled=True)]
    unnamed x14 -> x16, local copies, waits for them, and re-layouts: 11.5 us -> 12.2 us
  transfers between devices with their start and end apart: 8 -> 11, of which waited for: 8 -> 9; matrix products, arithmetic and copies ran while one was open for 0% -> 51% of each run, Pallas kernels for 0% -> 0%
where the time goes in v1:
time: 354 us; the launch traced here: 349 us
  matrix products  136 us (38%)
  waiting for transfers between devices  127 us (36%)
  local copies, waits for them, and re-layouts  40.2 us (11%)
  between operations  13.9 us (4%)
  blocking collectives  12.3 us (3%)
  starting transfers between devices  11.5 us (3%)
  other arithmetic  4.91 us (1%)
    reduce_scatter x1, waiting for transfers between devices, on_device(): lax.psum_scatter(lax.dot_general(gathered, adjoint_bf, (((0,), (1,)), (()...  89.4 us
    dot_general x32, matrix products, build_step(): jnp.einsum('hji,hjsk->hisk', block_weights, matrices, precision=exact)  49.1 us
    dot_general x32, matrix products, solve_step(): jnp.einsum('hji,hjs->his', block_weights, subsequent_step, precision=exact)  36.2 us
    dot_general x32, matrix products, build_step(): jnp.einsum('hji,hjs->his', block_weights, offsets, precision=exact)  35.6 us
    ppermute x7, waiting for transfers between devices, from_behind(): return lax.ppermute(value, axis, pairs)  34.3 us
    pad x6, local copies, waits for them, and re-layouts, on_device(): suffix = lax.associative_scan(compose, flipped, axis=2)  17.5 us
    all_to_all x1, blocking collectives, on_device(): lax.all_to_all(summed, 'tp', split_axis=0, concat_axis=1, tiled=True)  12.3 us
    unnamed x16, local copies, waits for them, and re-layouts  12.2 us
  transfers between devices with their start and end apart: 11, of which 9 were waited for; matrix products, arithmetic and copies ran while one was open for 51% of the time, Pallas kernels for 0%

profile of v1, /device:TPU:0, one launch (start us, length us, event | category | flops | bytes accessed | tf_op | source)
XLA Modules:
  0.0 348.5 jit_solution(13701894190722713472)
XLA Ops:
  6.5 2.4 collective-permute-start.2
  12.9 89.9 %while.45 = (s32[]{:T(128)}, f32[8,64,6,64]{3,1,2,0:T(8,128)S(1)}, f32[8,64,6]{1,2,0:T(8,128)S(1)}, f32[32,8,64,6]{2,3,1,0:T(8,128)S(1)}, f32[8,64,64]{2,1,0:T(8...) while((s32[]{:T(128)}, f32[8,64,6,64]{3,1,2,0:T(8,128)S(1)}, ...), condition=%wide.region_1.2_spmd.clone, body=%wide.region_0.1_spmd.clone.sunk | while | flops 153560064 | bytes 3518595 | solution.py:52
  16.9 1.5 convolution_multiply_fusion.2
  22.6 1.5 convolution_multiply_fusion.2
  28.2 1.5 convolution_multiply_fusion.2
  33.8 1.5 convolution_multiply_fusion.2
  39.4 1.5 convolution_multiply_fusion.2
  45.0 1.5 convolution_multiply_fusion.2
  67.5 1.5 convolution_multiply_fusion.2
  73.1 1.5 convolution_multiply_fusion.2
  78.7 1.5 convolution_multiply_fusion.2
  84.3 1.5 convolution_multiply_fusion.2
  90.0 1.5 convolution_multiply_fusion.2
  108.0 1.6 copy.17
  111.3 1.8 convolution_bitcast_fusion.1
  113.1 8.5 %pad.66 = f32[8,64,5,64]{1,3,2,0:T(8,128)} pad(f32[8,64,3,64]{1,3,2,0:T(8,128)S(1)} %pad_add_fusion, f32[]{:T(128)} %constant.121.clone.1), padding=0_0_0x0_0_0x0_0_1x0_0_0 | pad | bytes 1048580
  121.6 8.6 %pad.33 = f32[8,64,6,64]{1,3,2,0:T(8,128)} pad(f32[8,64,3,64]{1,3,2,0:T(8,128)S(1)} %pad_add_fusion, f32[]{:T(128)} %constant.121.clone.1), padding=0_0_0x0_0_0x1_0_1x0_0_0 | pad | bytes 1179652 | tf_op jit(solution)/shard_map/pad | solution.py:56
  132.4 8.5 %pad.32 = f32[8,64,6,64]{1,3,2,0:T(8,128)} pad(f32[8,64,3,64]{1,3,2,0:T(8,128)S(1)} %pad_maximum_fusion, f32[]{:T(128)} %constant.121.clone.1), padding=0_0_0x0_0_0x0_1_1x0_0_0 | pad | bytes 1179652 | tf_op jit(solution)/shard_map/pad | solution.py:56
  142.7 47.1 %while.43 = (s32[]{:T(128)}, f32[8,64,1]{1,0,2:T(8,128)S(1)}, f32[8,64,1]{1,2,0:T(1,128)S(1)}, f32[8,64,1,64]{3,2,1,0:T(1,128)S(1)}, s32[]{:T(128)}) while((s32[]{:T(128)}, f32[8,64,1]{1,0,2:T(8,128)S(1)}, f32[8,64,1]{1,2,0:T(1,128)S(1)}, f32[8,64,1,64]{3,2,1,0:T(1,128)S(1)}, s32[]{:T(128)}) %tuple.90), condition=%wide.region_3.4_spmd, body=%wide.region_2.3_spmd.sunk | while | flops 393730 | bytes 149605 | solution.py:66
  144.6 4.2 %collective-permute-done = f32[8,64,1]{1,0,2:T(8,128)S(1)} collective-permute-done((f32[8,64,1]{1,0,2:T(8,128)S(1)}, f32[8,64,1]{1,0,2:T(8,128)S(1)}, u32[]{:S(2)}, u32[]{:S(2)}) %collective-permute-start) | collective-permute-done | bytes 2080 | tf_op jit(solution)/shard_map/while/body/eval_jaxpr/ppermute | solution.py:12
  150.6 4.6 %collective-permute-done = f32[8,64,1]{1,0,2:T(8,128)S(1)} collective-permute-done((f32[8,64,1]{1,0,2:T(8,128)S(1)}, f32[8,64,1]{1,0,2:T(8,128)S(1)}, u32[]{:S(2)}, u32[]{:S(2)}) %collective-permute-start) | collective-permute-done | bytes 2080 | tf_op jit(solution)/shard_map/while/body/eval_jaxpr/ppermute | solution.py:12
  157.0 5.1 %collective-permute-done = f32[8,64,1]{1,0,2:T(8,128)S(1)} collective-permute-done((f32[8,64,1]{1,0,2:T(8,128)S(1)}, f32[8,64,1]{1,0,2:T(8,128)S(1)}, u32[]{:S(2)}, u32[]{:S(2)}) %collective-permute-start) | collective-permute-done | bytes 2080 | tf_op jit(solution)/shard_map/while/body/eval_jaxpr/ppermute | solution.py:12
  163.9 5.1 %collective-permute-done = f32[8,64,1]{1,0,2:T(8,128)S(1)} collective-permute-done((f32[8,64,1]{1,0,2:T(8,128)S(1)}, f32[8,64,1]{1,0,2:T(8,128)S(1)}, u32[]{:S(2)}, u32[]{:S(2)}) %collective-permute-start) | collective-permute-done | bytes 2080 | tf_op jit(solution)/shard_map/while/body/eval_jaxpr/ppermute | solution.py:12
  170.8 5.1 %collective-permute-done = f32[8,64,1]{1,0,2:T(8,128)S(1)} collective-permute-done((f32[8,64,1]{1,0,2:T(8,128)S(1)}, f32[8,64,1]{1,0,2:T(8,128)S(1)}, u32[]{:S(2)}, u32[]{:S(2)}) %collective-permute-start) | collective-permute-done | bytes 2080 | tf_op jit(solution)/shard_map/while/body/eval_jaxpr/ppermute | solution.py:12
  177.8 5.1 %collective-permute-done = f32[8,64,1]{1,0,2:T(8,128)S(1)} collective-permute-done((f32[8,64,1]{1,0,2:T(8,128)S(1)}, f32[8,64,1]{1,0,2:T(8,128)S(1)}, u32[]{:S(2)}, u32[]{:S(2)}) %collective-permute-start) | collective-permute-done | bytes 2080 | tf_op jit(solution)/shard_map/while/body/eval_jaxpr/ppermute | solution.py:12
  184.7 5.1 %collective-permute-done = f32[8,64,1]{1,0,2:T(8,128)S(1)} collective-permute-done((f32[8,64,1]{1,0,2:T(8,128)S(1)}, f32[8,64,1]{1,0,2:T(8,128)S(1)}, u32[]{:S(2)}, u32[]{:S(2)}) %collective-permute-start) | collective-permute-done | bytes 2080 | tf_op jit(solution)/shard_map/while/body/eval_jaxpr/ppermute | solution.py:12
  189.8 2.2 fusion.24
  192.8 37.2 %while.44 = (s32[]{:T(128)}, f32[8,64,6]{1,2,0:T(8,128)S(1)}, bf16[32,8,64,6]{2,3,1,0:T(8,128)(2,1)S(1)}, f32[32,8,64,6]{2,3,1,0:T(8,128)}, f32[32,8,64,6]{2,3,1...) while((s32[]{:T(128)}, f32[8,64,6]{1,2,0:T(8,128)S(1)}, ...), condition=%wide.region_5.6_spmd, body=%wide.region_4.5_spmd.sunk | while | flops 2365443 | bytes 409701 | solution.py:81
  233.0 3.4 collective-permute-done.3
  236.4 2.7 fusion.25
  239.1 89.4 %reduce-scatter.2.cloned.1.call-done = f32[256,512]{1,0:T(8,128)} async-done(((f32[2048,512]{1,0:T(8,128)}), f32[256,512]{1,0:T(8,128)}) %reduce-scatter.2.cloned.1.call-update) | async-done | bytes 524304 | tf_op jit(solution)/shard_map/reduce_scatter | solution.py:107
  328.6 12.3 %all_to_all.19 = f32[4,64,512]{2,1,0:T(8,128)S(1)} all-to-all(f32[4,64,512]{2,1,0:T(8,128)} %bitcast.156), channel_id=1, replica_groups=mesh['ctx'=8,'tp'=4] {'tp'}, dimensions={0} | all-to-all | bytes 1048576 | tf_op jit(solution)/shard_map/all_to_all | solution.py:115
  (315 shorter events, 139.7 us)
Async XLA Ops:
  6.5 322.0 %reduce-scatter.2.cloned.1.call-start = ((), (), s32[]{:S(2)}) async-start(), calls=%async_computation.2 | async-start | bytes 4718592 | tf_op jit(solution)/shard_map/reduce_scatter | solution.py:107
  6.5 225.5 %collective-permute-start.2 = (bf16[192,512]{1,0:T(8,128)(2,1)}, bf16[192,512]{1,0:T(8,128)(2,1)}, u32[]{:S(2)}, u32[]{:S(2)}) collective-permute-start(bf16[192,512]{1,0:T(8,128)(2,1)} %param.10), channel_id=1, source_target_pairs={{0,3},{1,0},{2,1},{3,2},{4,7},{5,4},{6,5},{7,6},{8,11},{9,8},{10,9... | collective-permute-start | bytes 589832 | tf_op jit(solution)/shard_map/ppermute | solution.py:101
  8.9 222.1 %collective-permute-start.1 = (bf16[192,512]{1,0:T(8,128)(2,1)}, bf16[192,512]{1,0:T(8,128)(2,1)}, u32[]{:S(2)}, u32[]{:S(2)}) collective-permute-start(bf16[192,512]{1,0:T(8,128)(2,1)} %param.10), channel_id=1, source_target_pairs={{0,1},{1,2},{2,3},{3,0},{4,5},{5,6},{6,7},{7,4},{8,9},{9,10},{10,1... | collective-permute-start | bytes 589832 | tf_op jit(solution)/shard_map/ppermute | solution.py:94
  10.0 1.0 copy-start.4
  11.1 1.7 copy-start
  102.7 1.0 copy-start.3
  108.0 2.0 copy-start.2
  121.6 9.7 %slice-start = ((f32[8,64,6,64]{1,3,2,0:T(8,128)}), f32[8,64,1,64]{1,3,2,0:T(8,128)S(1)}, s32[]{:S(2)}) async-start(f32[8,64,6,64]{1,3,2,0:T(8,128)} %copy.17), calls=%async_computation.3 | async-start | bytes 524288 | tf_op jit(solution)/shard_map/slice | solution.py:56
  132.4 8.5 %slice-start.1 = ((f32[8,64,5,64]{1,3,2,0:T(8,128)}), f32[8,64,1,64]{1,3,2,0:T(8,128)S(1)}, s32[]{:S(2)}) async-start(f32[8,64,5,64]{1,3,2,0:T(8,128)} %pad.66), calls=%async_computation.4 | async-start | bytes 524288 | tf_op jit(solution)/shard_map/slice | solution.py:59
  132.4 8.7 %copy-start.1 = (f32[8,64,6,64]{1,3,2,0:T(8,128)S(1)}, f32[8,64,6,64]{1,3,2,0:T(8,128)}, u32[]{:S(2)}) copy-start(f32[8,64,6,64]{1,3,2,0:T(8,128)} %pad.33) | copy-start | bytes 2359300
  143.3 5.5 %collective-permute-start = (f32[8,64,1]{1,0,2:T(8,128)S(1)}, f32[8,64,1]{1,0,2:T(8,128)S(1)}, u32[]{:S(2)}, u32[]{:S(2)}) collective-permute-start(f32[8,64,1]{1,0,2:T(8,128)S(1)} %add_bitcast_fusion.2), channel_id=1, source_target_pairs={{4,0},{8,4},{12,8},{16,12},{20,16},{24,20},{28,24},{5,1},{9,5},{13... | collective-permute-start | bytes 6152 | tf_op jit(solution)/shard_map/while/body/eval_jaxpr/ppermute | solution.py:12
  149.3 5.9 %collective-permute-start = (f32[8,64,1]{1,0,2:T(8,128)S(1)}, f32[8,64,1]{1,0,2:T(8,128)S(1)}, u32[]{:S(2)}, u32[]{:S(2)}) collective-permute-start(f32[8,64,1]{1,0,2:T(8,128)S(1)} %add_bitcast_fusion.2), channel_id=1, source_target_pairs={{4,0},{8,4},{12,8},{16,12},{20,16},{24,20},{28,24},{5,1},{9,5},{13... | collective-permute-start | bytes 6152 | tf_op jit(solution)/shard_map/while/body/eval_jaxpr/ppermute | solution.py:12
  155.7 6.4 %collective-permute-start = (f32[8,64,1]{1,0,2:T(8,128)S(1)}, f32[8,64,1]{1,0,2:T(8,128)S(1)}, u32[]{:S(2)}, u32[]{:S(2)}) collective-permute-start(f32[8,64,1]{1,0,2:T(8,128)S(1)} %add_bitcast_fusion.2), channel_id=1, source_target_pairs={{4,0},{8,4},{12,8},{16,12},{20,16},{24,20},{28,24},{5,1},{9,5},{13... | collective-permute-start | bytes 6152 | tf_op jit(solution)/shard_map/while/body/eval_jaxpr/ppermute | solution.py:12
  162.6 6.4 %collective-permute-start = (f32[8,64,1]{1,0,2:T(8,128)S(1)}, f32[8,64,1]{1,0,2:T(8,128)S(1)}, u32[]{:S(2)}, u32[]{:S(2)}) collective-permute-start(f32[8,64,1]{1,0,2:T(8,128)S(1)} %add_bitcast_fusion.2), channel_id=1, source_target_pairs={{4,0},{8,4},{12,8},{16,12},{20,16},{24,20},{28,24},{5,1},{9,5},{13... | collective-permute-start | bytes 6152 | tf_op jit(solution)/shard_map/while/body/eval_jaxpr/ppermute | solution.py:12
  169.5 6.4 %collective-permute-start = (f32[8,64,1]{1,0,2:T(8,128)S(1)}, f32[8,64,1]{1,0,2:T(8,128)S(1)}, u32[]{:S(2)}, u32[]{:S(2)}) collective-permute-start(f32[8,64,1]{1,0,2:T(8,128)S(1)} %add_bitcast_fusion.2), channel_id=1, source_target_pairs={{4,0},{8,4},{12,8},{16,12},{20,16},{24,20},{28,24},{5,1},{9,5},{13... | collective-permute-start | bytes 6152 | tf_op jit(solution)/shard_map/while/body/eval_jaxpr/ppermute | solution.py:12
  176.5 6.4 %collective-permute-start = (f32[8,64,1]{1,0,2:T(8,128)S(1)}, f32[8,64,1]{1,0,2:T(8,128)S(1)}, u32[]{:S(2)}, u32[]{:S(2)}) collective-permute-start(f32[8,64,1]{1,0,2:T(8,128)S(1)} %add_bitcast_fusion.2), channel_id=1, source_target_pairs={{4,0},{8,4},{12,8},{16,12},{20,16},{24,20},{28,24},{5,1},{9,5},{13... | collective-permute-start | bytes 6152 | tf_op jit(solution)/shard_map/while/body/eval_jaxpr/ppermute | solution.py:12
  183.4 6.4 %collective-permute-start = (f32[8,64,1]{1,0,2:T(8,128)S(1)}, f32[8,64,1]{1,0,2:T(8,128)S(1)}, u32[]{:S(2)}, u32[]{:S(2)}) collective-permute-start(f32[8,64,1]{1,0,2:T(8,128)S(1)} %add_bitcast_fusion.2), channel_id=1, source_target_pairs={{4,0},{8,4},{12,8},{16,12},{20,16},{24,20},{28,24},{5,1},{9,5},{13... | collective-permute-start | bytes 6152 | tf_op jit(solution)/shard_map/while/body/eval_jaxpr/ppermute | solution.py:12
  230.1 0.9 copy-start.5
  231.0 5.4 %collective-permute-start.3 = (bf16[192,512]{1,0:T(8,128)(2,1)}, bf16[192,512]{1,0:T(8,128)(2,1)S(1)}, u32[]{:S(2)}, u32[]{:S(2)}) collective-permute-start(bf16[192,512]{1,0:T(8,128)(2,1)} %collective-permute-done.1), channel_id=1, source_target_pairs={{0,1},{1,2},{2,3},{3,0},{4,5},{5,6},{6,7},{7,4},{8,9},{9,10},{10,1... | collective-permute-start | bytes 589832 | tf_op jit(solution)/shard_map/ppermute | solution.py:94
Sparse Core Ops, SparseCore 0:
  239.3 89.2 reduce-scatter.1
